TPU v7x, 128 devices: a whole 4x4x4 slice. The times are simulated.
128 devices in a mesh: seq: 16 (over y_lo, x, core), cb: 8 (over y_hi, z).
Axes of the slice: x: 4, y: 4 (y_hi: 2, y_lo: 2; y = y_hi * 2 + y_lo), z: 4, core: 2. Of those that a mesh axis runs over, the one named last changes fastest.
Arguments:
- hidden: bfloat16 [2, 2048, 4096], P(None, 'seq'), may hold values from -6 to 6
- temporal_gain: float32 [4096], replicated, may hold values from 0.5 to 2
- temporal_qkv: bfloat16 [3, 4096, 2048], P(None, None, 'cb'), may hold values from -10 to 10
- temporal_out: bfloat16 [2048, 4096], P('cb'), may hold values from -0.125 to 0.125
- codebook_ids: int32 [2, 2048, 8], P(None, 'seq', 'cb'), may hold values from 0 to 2047
- embedding: bfloat16 [8, 2048, 1024], P('cb'), may hold values from -6 to 6
- input_weight: bfloat16 [8, 4096, 1024], P('cb', 'seq'), may hold values from -0.09375 to 0.09375
- depth_gain: float32 [8, 1024], P('cb'), may hold values from 0.5 to 2
- depth_qkv: bfloat16 [8, 3, 1024, 1024], P('cb'), may hold values from -10 to 10
- depth_out: bfloat16 [8, 1024, 1024], P('cb'), may hold values from -0.1875 to 0.1875
Outputs:
- temporal: bfloat16 [2, 2048, 4096], P(None, 'seq')
- depth: bfloat16 [2, 2048, 8, 1024], P(None, 'seq', 'cb')
All inputs are finite; a program needn't handle non-finite values.
Results may differ from a plain program's by a relative error of at most 0.017.
Values may be sent and summed in bfloat16 or wider, within the bound.
A program may use at most 128 MiB of HBM per device.

v0:
```python
import jax
import jax.numpy as jnp
from jax import lax
from jax.sharding import PartitionSpec as P

HD = 128
DW = 1024
DH = 16
DHD = 64


def normalize(values, scale):
    mean_sq = jnp.mean(values * values, axis=-1, keepdims=True)
    return values * lax.rsqrt(mean_sq + 1e-05) * scale


def shards(
    hidden,
    temporal_gain,
    temporal_qkv,
    temporal_out,
    codebook_ids,
    embedding,
    input_weight,
    depth_gain,
    depth_qkv,
    depth_out,
):
    seq_count, frames, width = hidden.shape
    head_cols = temporal_qkv.shape[2]
    head_count = head_cols // HD
    row_count = seq_count * frames
    hidden_f = hidden.astype(jnp.float32)
    normed = normalize(hidden_f, temporal_gain).astype(jnp.bfloat16).reshape(row_count, width)
    projected = []
    for which in range(3):
        part_rows = jnp.dot(normed, temporal_qkv[which], preferred_element_type=jnp.float32).astype(
            jnp.bfloat16
        )
        projected.append(part_rows.reshape(seq_count, frames, head_count, HD))
    queries = projected[0]
    query_pos = lax.axis_index("seq") * frames + jnp.arange(frames, dtype=jnp.int32)
    temporal_scale = 1.0 / jnp.sqrt(jnp.float32(HD))
    highest = jnp.full((seq_count, head_count, frames), -1e30, jnp.float32)
    key_piece = lax.all_gather(projected[1], "seq", axis=1, tiled=True)
    value_piece = lax.all_gather(projected[2], "seq", axis=1, tiled=True)
    count = key_piece.shape[1]
    scores = (
        jnp.einsum("sqhd,skhd->shqk", queries, key_piece, preferred_element_type=jnp.float32)
        * temporal_scale
    )
    key_pos = jnp.arange(count, dtype=jnp.int32)
    allowed = (key_pos[None, :] <= query_pos[:, None])[None, None]
    scores = jnp.where(allowed, scores, -1e30)
    new_high = jnp.maximum(highest, jnp.max(scores, axis=-1))
    weights = jnp.where(allowed, jnp.exp(scores - new_high[..., None]), 0.0)
    totals = jnp.sum(weights, axis=-1)
    update = jnp.einsum(
        "shqk,skhd->sqhd",
        weights.astype(jnp.bfloat16),
        value_piece,
        preferred_element_type=jnp.float32,
    )
    gathered = update
    highest, totals, gathered = (new_high, totals, gathered)
    mixed = (
        (gathered / totals.transpose(0, 2, 1)[..., None])
        .astype(jnp.bfloat16)
        .reshape(row_count, head_cols)
    )
    term = jnp.dot(mixed, temporal_out, preferred_element_type=jnp.float32)
    summed = lax.psum(term.astype(jnp.bfloat16), "cb").astype(jnp.float32)
    temporal = (hidden_f.reshape(row_count, width) + summed).astype(jnp.bfloat16)
    projected_in = jnp.dot(
        temporal,
        lax.all_gather(input_weight, "seq", axis=1, tiled=True)[0],
        preferred_element_type=jnp.float32,
    )
    entry = jnp.take(embedding[0], codebook_ids.reshape(row_count), axis=0).astype(jnp.float32)
    stream = (projected_in + entry).astype(jnp.bfloat16)
    depth_normed = normalize(stream.astype(jnp.float32), depth_gain[0]).astype(jnp.bfloat16)
    book_query = jnp.dot(depth_normed, depth_qkv[0, 0], preferred_element_type=jnp.float32).astype(
        jnp.bfloat16
    )
    book_key = jnp.dot(depth_normed, depth_qkv[0, 1], preferred_element_type=jnp.float32).astype(
        jnp.bfloat16
    )
    book_value = jnp.dot(depth_normed, depth_qkv[0, 2], preferred_element_type=jnp.float32).astype(
        jnp.bfloat16
    )
    depth_scale = 1.0 / jnp.sqrt(jnp.float32(DHD))
    my_book = lax.axis_index("cb")
    query_heads = book_query.reshape(row_count, DH, DHD)
    highest_b = jnp.full((row_count, DH), -1e30, jnp.float32)
    key_piece = lax.all_gather(book_key[None], "cb", axis=0, tiled=True)
    value_piece = lax.all_gather(book_value[None], "cb", axis=0, tiled=True)
    count = key_piece.shape[0]
    key_heads = key_piece.reshape(count, row_count, DH, DHD)
    value_heads = value_piece.reshape(count, row_count, DH, DHD)
    scores = (
        jnp.einsum("rhd,jrhd->rhj", query_heads, key_heads, preferred_element_type=jnp.float32)
        * depth_scale
    )
    permitted = (jnp.arange(count, dtype=jnp.int32) <= my_book)[None, None, :]
    scores = jnp.where(permitted, scores, -1e30)
    new_high = jnp.maximum(highest_b, jnp.max(scores, axis=-1))
    weights = jnp.where(permitted, jnp.exp(scores - new_high[..., None]), 0.0)
    totals_b = jnp.sum(weights, axis=-1)
    update = jnp.einsum(
        "rhj,jrhd->rhd",
        weights.astype(jnp.bfloat16),
        value_heads,
        preferred_element_type=jnp.float32,
    )
    highest_b, totals_b, gathered_b = (new_high, totals_b, update)
    book_mixed = (gathered_b / totals_b[..., None]).astype(jnp.bfloat16).reshape(row_count, DW)
    depth = (
        jnp.dot(book_mixed, depth_out[0], preferred_element_type=jnp.float32)
        + stream.astype(jnp.float32)
    ).astype(jnp.bfloat16)
    return (temporal.reshape(seq_count, frames, width), depth.reshape(seq_count, frames, 1, DW))


def solution(mesh):
    placed = (
        P(None, "seq", None),
        P(),
        P(None, None, "cb"),
        P("cb", None),
        P(None, "seq", "cb"),
        P("cb", None, None),
        P("cb", "seq", None),
        P("cb", None),
        P("cb", None, None, None),
        P("cb", None, None),
    )
    return jax.shard_map(
        shards,
        mesh=mesh,
        in_specs=placed,
        out_specs=(P(None, "seq", None), P(None, "seq", "cb", None)),
        check_vma=False,
    )
```

profile of v0, /device:TPU:1, one launch (start us, length us, event | category | flops | bytes accessed | tf_op | source)
XLA Modules:
  0.0 419.6 jit_solution(1029900267491474171)
XLA Ops:
  7.2 2.2 multiply_reduce_fusion.2
  9.5 2.3 multiply_convert_fusion
  13.1 2.3 fusion.58
  16.3 2.9 fusion.52
  20.1 2.9 fusion.55
  23.3 30.6 %all-gather.10.cloned.1.call-done = bf16[2,2048,2,128]{3,1,2,0:T(8,128)(2,1)} async-done(((bf16[2,128,2,128]{3,1,2,0:T(8,128)(2,1)}), bf16[2,2048,2,128]{3,1,2,0:T(8,128)(2,1)}) %all-gather.10.cloned.1.call-update) | async-done | bytes 2097168 | tf_op jit(solution)/shard_map/all_gather | solution.py:45
  53.9 2.6 fusion.3
  59.7 33.6 %all-gather.8.cloned.1.call-done = bf16[2,2048,2,128]{1,3,2,0:T(8,128)(2,1)} async-done(((bf16[2,128,2,128]{1,3,2,0:T(8,128)(2,1)}), bf16[2,2048,2,128]{1,3,2,0:T(8,128)(2,1)}) %all-gather.8.cloned.1.call-update) | async-done | bytes 2097168 | tf_op jit(solution)/shard_map/all_gather | solution.py:46
  93.4 4.1 fusion.64
  100.6 4.3 %gather_fusion = bf16[256,1024]{1,0:T(8,128)(2,1)S(1)} fusion(bf16[2048,1024]{1,0:T(8,128)(2,1)} %bitcast.102, s32[1024]{0:T(1024)S(1)} %pad_clamp_fusion), kind=kCustom, calls=%fused_computation | custom fusion | bytes 1049600 | tf_op jit(solution)/shard_map/jit(_take)/gather | solution.py:79
  104.9 82.8 %all-reduce.2.cloned.1.call-done = bf16[256,4096]{1,0:T(8,128)(2,1)} async-done(((bf16[256,4096]{1,0:T(8,128)(2,1)}), bf16[256,4096]{1,0:T(8,128)(2,1)}) %all-reduce.2.cloned.1.call-update) | async-done | bytes 2097168 | tf_op jit(solution)/shard_map/psum | solution.py:72
  187.7 3.7 fusion.2
  191.4 53.9 %all-gather.12.cloned.1.call-done = bf16[1,4096,1024]{2,1,0:T(8,128)(2,1)} async-done(((bf16[1,256,1024]{2,1,0:T(8,128)(2,1)}), bf16[1,4096,1024]{2,1,0:T(8,128)(2,1)}) %all-gather.12.cloned.1.call-update) | async-done | bytes 8388624 | tf_op jit(solution)/shard_map/all_gather | solution.py:76
  245.2 6.5 %fusion.67 = (f32[256]{0:T(256)S(1)}, bf16[256,1024]{1,0:T(8,128)(2,1)S(1)}) fusion(bf16[256,1024]{1,0:T(8,128)(2,1)S(1)} %gather_fusion, pred[256]{0:T(512)(128)(4,1)S(1)} %compare_and_fusion, bf16[256,4096]{1,0:T(8,128)(2,1)} %fusion.2, bf16[1,4096,1024]{2,1,0:T(8,128)(2,1)} %all-gather.12.cloned.1.call-done), kind=kOutput, calls=%fused_computation.52 | convolution fusion | flops 2149318400 | bytes 11535616 | tf_op jit(solution)/shard_map/dot_general | solution.py:74
  251.7 3.1 fusion.43
  255.1 3.2 fusion.46
  258.4 2.4 fusion.40
  261.1 65.6 %all-gather.14.cloned.1.call-done = bf16[2048,1024]{1,0:T(8,128)(2,1)} async-done(((bf16[256,1024]{1,0:T(8,128)(2,1)}), bf16[2048,1024]{1,0:T(8,128)(2,1)}) %all-gather.14.cloned.1.call-update) | async-done | bytes 4194320 | tf_op jit(solution)/shard_map/all_gather | solution.py:95
  326.7 6.5 %copy.29 = bf16[2048,1024]{0,1:T(8,128)(2,1)} copy(bf16[2048,1024]{1,0:T(8,128)(2,1)} %all-gather.14.cloned.1.call-done) | data formatting | bytes 8388608 | tf_op jit(solution)/shard_map/all_gather | solution.py:95
  333.1 3.7 copy.47
  338.0 60.2 %all-gather.16.cloned.1.call-done = bf16[2048,1024]{1,0:T(8,128)(2,1)} async-done(((bf16[256,1024]{1,0:T(8,128)(2,1)}), bf16[2048,1024]{1,0:T(8,128)(2,1)}) %all-gather.16.cloned.1.call-update) | async-done | bytes 4194320 | tf_op jit(solution)/shard_map/all_gather | solution.py:96
  398.2 6.5 %copy.30 = bf16[2048,1024]{0,1:T(8,128)(2,1)} copy(bf16[2048,1024]{1,0:T(8,128)(2,1)} %all-gather.16.cloned.1.call-done) | data formatting | bytes 8388608 | tf_op jit(solution)/shard_map/all_gather | solution.py:96
  404.7 3.7 copy.48
  408.4 2.6 multiply_reduce_fusion
  (53 shorter events, 12.9 us)
Async XLA Ops:
  7.2 90.5 %copy-start = (bf16[256,4096]{1,0:T(8,128)(2,1)S(1)}, bf16[256,4096]{1,0:T(8,128)(2,1)}, u32[]{:S(2)}) copy-start(bf16[256,4096]{1,0:T(8,128)(2,1)} %param.13) | copy-start | bytes 6291460
  7.2 46.7 %all-gather.10.cloned.1.call-start = ((), (), s32[]{:S(2)}) async-start(), calls=%async_computation.1 | async-start | bytes 2228224 | tf_op jit(solution)/shard_map/all_gather | solution.py:45
  11.8 1.3 copy-start.5
  16.2 77.2 %all-gather.8.cloned.1.call-start = ((), (), s32[]{:S(2)}) async-start(), calls=%async_computation | async-start | bytes 2228224 | tf_op jit(solution)/shard_map/all_gather | solution.py:46
  20.0 167.7 %all-reduce.2.cloned.1.call-start = ((), (), s32[]{:S(2)}) async-start(), calls=%async_computation.2 | async-start | bytes 4194304 | tf_op jit(solution)/shard_map/psum | solution.py:72
  56.5 1.9 copy-start.3
  97.5 3.0 copy-start.6
  99.7 88.0 %copy-start.2 = (bf16[2,128,4096]{2,1,0:T(8,128)(2,1)S(1)}, bf16[2,128,4096]{2,1,0:T(8,128)(2,1)}, u32[]{:S(2)}) copy-start(bf16[2,128,4096]{2,1,0:T(8,128)(2,1)} %param.10) | copy-start | bytes 6291460
  99.7 145.5 %all-gather.12.cloned.1.call-start = ((), (), s32[]{:S(2)}) async-start(), calls=%async_computation.3 | async-start | bytes 8912896 | tf_op jit(solution)/shard_map/all_gather | solution.py:76
  100.3 226.4 %all-gather.14.cloned.1.call-start = ((), (), s32[]{:S(2)}) async-start(), calls=%async_computation.4 | async-start | bytes 4718592 | tf_op jit(solution)/shard_map/all_gather | solution.py:95
  191.4 60.3 %copy-start.7 = (f32[1,1024]{1,0:T(1,128)S(1)}, f32[1,1024]{1,0:T(1,128)}, u32[]{:S(2)}) copy-start(f32[1,1024]{1,0:T(1,128)} %param.17) | copy-start | bytes 12292
  254.9 143.3 %all-gather.16.cloned.1.call-start = ((), (), s32[]{:S(2)}) async-start(), calls=%async_computation.5 | async-start | bytes 4718592 | tf_op jit(solution)/shard_map/all_gather | solution.py:96
  408.4 2.8 copy-start.4
  408.4 4.3 %copy-start.1 = (bf16[256,4096]{1,0:T(8,128)(2,1)S(1)}, bf16[256,4096]{1,0:T(8,128)(2,1)}, u32[]{:S(2)}) copy-start(bf16[256,4096]{1,0:T(8,128)(2,1)} %param.13) | copy-start | bytes 6291460
Sparse Core Ops, SparseCore 0:
  16.3 37.5 all-gather.9
  56.1 37.2 all-gather.7
  99.8 87.8 all-reduce.1
  189.2 55.9 all-gather.11
  255.0 71.6 all-gather.13
  328.9 69.2 all-gather.15
where the time goes:
time: 420 us
  waiting for transfers between devices  327 us (78%)
  matrix products  33.6 us (8%)
  local copies, waits for them, and re-layouts  29.8 us (7%)
  between operations  14.4 us (3%)
  other arithmetic  13.8 us (3%)
    psum x1, waiting for transfers between devices, shards(): summed = lax.psum(term.astype(jnp.bfloat16), 'cb').astype(jnp.float32)  82.8 us
    all_gather x1, waiting for transfers between devices, shards(): key_piece = lax.all_gather(book_key[None], 'cb', axis=0, tiled=True)  65.6 us
    all_gather x1, waiting for transfers between devices, shards(): value_piece = lax.all_gather(book_value[None], 'cb', axis=0, tiled=True)  60.2 us
    all_gather x1, waiting for transfers between devices, shards(): lax.all_gather(input_weight, 'seq', axis=1, tiled=True)[0]  53.9 us
    all_gather x1, waiting for transfers between devices, shards(): value_piece = lax.all_gather(projected[2], 'seq', axis=1, tiled=True)  33.6 us
    all_gather x1, waiting for transfers between devices, shards(): key_piece = lax.all_gather(projected[1], 'seq', axis=1, tiled=True)  30.6 us
    unnamed x18, local copies, waits for them, and re-layouts  10.6 us
  transfers between devices with their start and end apart: 6, of which 6 were waited for; matrix products, arithmetic and copies ran while one was open for 9% of the time, Pallas kernels for 0%

commit v1 on v0

--- a/solution.py
+++ b/solution.py
@@ -73,7 +73,9 @@
     temporal = (hidden_f.reshape(row_count, width) + summed).astype(jnp.bfloat16)
     projected_in = jnp.dot(
         temporal,
-        lax.all_gather(input_weight, "seq", axis=1, tiled=True)[0],
+        jnp.concatenate(
+            lax.all_to_all(jnp.stack([input_weight] * lax.axis_size("seq")), "seq", 0, 0), axis=1
+        )[0],
         preferred_element_type=jnp.float32,
     )
     entry = jnp.take(embedding[0], codebook_ids.reshape(row_count), axis=0).astype(jnp.float32)

time: 420 us -> 439 us (1.045)
  waiting for transfers between devices: 327 us -> 335 us
  starting transfers between devices: 0.65 us -> 7.21 us
  local copies, waits for them, and re-layouts: 29.8 us -> 34.2 us
    all_gather x1 -> x0, waiting for transfers between devices: 53.9 us -> none  [shards(): lax.all_gather(input_weight, 'seq', axis=1, tiled=True)[0]]
    all_gather x1, waiting for transfers between devices: 33.6 us -> 67.7 us  [shards(): value_piece = lax.all_gather(projected[2], 'seq', axis=1, tiled=True)]
    all_gather x1, waiting for transfers between devices: 30.6 us -> 53.3 us  [shards(): key_piece = lax.all_gather(projected[1], 'seq', axis=1, tiled=True)]
    all_to_all x0 -> x1, starting transfers between devices: none -> 6.83 us  [shards(): lax.all_to_all(jnp.stack([input_weight] * lax.axis_size('seq')), 'seq', 0...]
    unnamed x18 -> x20, local copies, waits for them, and re-layouts: 10.6 us -> 10.6 us
  transfers between devices with their start and end apart: 6 -> 6, of which waited for: 6 -> 5; matrix products, arithmetic and copies ran while one was open for 9% -> 11% of each run, Pallas kernels for 0% -> 0%
where the time goes in v1:
time: 439 us; the launch traced here: 438 us
  waiting for transfers between devices  335 us (76%)
  local copies, waits for them, and re-layouts  34.2 us (8%)
  matrix products  33.7 us (8%)
  between operations  14.1 us (3%)
  other arithmetic  13.8 us (3%)
  starting transfers between devices  7.21 us (2%)
    psum x1, waiting for transfers between devices, shards(): summed = lax.psum(term.astype(jnp.bfloat16), 'cb').astype(jnp.float32)  85.2 us
    all_gather x1, waiting for transfers between devices, shards(): key_piece = lax.all_gather(book_key[None], 'cb', axis=0, tiled=True)  68.8 us
    all_gather x1, waiting for transfers between devices, shards(): value_piece = lax.all_gather(projected[2], 'seq', axis=1, tiled=True)  67.7 us
    all_gather x1, waiting for transfers between devices, shards(): value_piece = lax.all_gather(book_value[None], 'cb', axis=0, tiled=True)  60.2 us
    all_gather x1, waiting for transfers between devices, shards(): key_piece = lax.all_gather(projected[1], 'seq', axis=1, tiled=True)  53.3 us
    unnamed x20, local copies, waits for them, and re-layouts  10.6 us
  transfers between devices with their start and end apart: 6, of which 5 were waited for; matrix products, arithmetic and copies ran while one was open for 11% of the time, Pallas kernels for 0%

profile of v1, /device:TPU:1, one launch (start us, length us, event | category | flops | bytes accessed | tf_op | source)
XLA Modules:
  0.0 438.3 jit_solution(11068968222931135475)
XLA Ops:
  9.5 2.3 multiply_convert_fusion
  13.1 2.3 fusion.51
  16.3 2.9 fusion.45
  20.0 4.3 stack.2
  24.4 6.8 %all-to-all-start = ((bf16[16,1,256,1024]{3,2,1,0:T(8,128)(2,1)}), bf16[16,1,256,1024]{3,2,1,0:T(8,128)(2,1)}, u32[]{:S(2)}, u32[]{:S(2)}) async-start(bf16[16,1,256,1024]{3,2,1,0:T(8,128)(2,1)} %stack.2), calls=%async_computation | async-start | bytes 16777216 | tf_op jit(solution)/shard_map/all_to_all | solution.py:77
  31.2 3.0 fusion.48
  34.5 53.3 %all-gather.9.cloned.1.call-done = bf16[2,2048,2,128]{3,1,2,0:T(8,128)(2,1)} async-done(((bf16[2,128,2,128]{3,1,2,0:T(8,128)(2,1)}), bf16[2,2048,2,128]{3,1,2,0:T(8,128)(2,1)}) %all-gather.9.cloned.1.call-update) | async-done | bytes 2097168 | tf_op jit(solution)/shard_map/all_gather | solution.py:45
  87.8 2.6 fusion.1
  93.6 67.7 %all-gather.7.cloned.1.call-done = bf16[2,2048,2,128]{1,3,2,0:T(8,128)(2,1)} async-done(((bf16[2,128,2,128]{1,3,2,0:T(8,128)(2,1)}), bf16[2,2048,2,128]{1,3,2,0:T(8,128)(2,1)}) %all-gather.7.cloned.1.call-update) | async-done | bytes 2097168 | tf_op jit(solution)/shard_map/all_gather | solution.py:46
  161.4 4.1 fusion.57
  168.0 4.4 %gather_fusion = bf16[256,1024]{1,0:T(8,128)(2,1)S(1)} fusion(bf16[2048,1024]{1,0:T(8,128)(2,1)} %bitcast.96, s32[1024]{0:T(1024)S(1)} %pad_clamp_fusion), kind=kCustom, calls=%fused_computation | custom fusion | bytes 1049600 | tf_op jit(solution)/shard_map/jit(_take)/gather | solution.py:81
  172.4 85.2 %all-reduce.2.cloned.1.call-done = bf16[256,4096]{1,0:T(8,128)(2,1)} async-done(((bf16[256,4096]{1,0:T(8,128)(2,1)}), bf16[256,4096]{1,0:T(8,128)(2,1)}) %all-reduce.2.cloned.1.call-update) | async-done | bytes 2097168 | tf_op jit(solution)/shard_map/psum | solution.py:72
  257.6 3.7 fusion
  261.3 6.5 %fusion.60 = (f32[256]{0:T(256)S(1)}, bf16[256,1024]{1,0:T(8,128)(2,1)S(1)}) fusion(bf16[256,1024]{1,0:T(8,128)(2,1)S(1)} %gather_fusion, pred[256]{0:T(512)(128)(4,1)S(1)} %compare_and_fusion, bf16[256,4096]{1,0:T(8,128)(2,1)} %fusion, bf16[4096,1024]{1,0:T(8,128)(2,1)} %bitcast.11), kind=kOutput, calls=%fused_computation.50 | convolution fusion | flops 2149318400 | bytes 11535616 | tf_op jit(solution)/shard_map/dot_general | solution.py:74
  267.8 3.1 fusion.36
  271.0 3.2 fusion.39
  274.2 2.3 fusion.33
  276.9 68.8 %all-gather.11.cloned.1.call-done = bf16[2048,1024]{1,0:T(8,128)(2,1)} async-done(((bf16[256,1024]{1,0:T(8,128)(2,1)}), bf16[2048,1024]{1,0:T(8,128)(2,1)}) %all-gather.11.cloned.1.call-update) | async-done | bytes 4194320 | tf_op jit(solution)/shard_map/all_gather | solution.py:97
  345.7 6.5 %copy.29 = bf16[2048,1024]{0,1:T(8,128)(2,1)} copy(bf16[2048,1024]{1,0:T(8,128)(2,1)} %all-gather.11.cloned.1.call-done) | data formatting | bytes 8388608 | tf_op jit(solution)/shard_map/all_gather | solution.py:97
  352.2 3.7 copy.47
  357.1 60.2 %all-gather.13.cloned.1.call-done = bf16[2048,1024]{1,0:T(8,128)(2,1)} async-done(((bf16[256,1024]{1,0:T(8,128)(2,1)}), bf16[2048,1024]{1,0:T(8,128)(2,1)}) %all-gather.13.cloned.1.call-update) | async-done | bytes 4194320 | tf_op jit(solution)/shard_map/all_gather | solution.py:98
  417.3 6.5 %copy.30 = bf16[2048,1024]{0,1:T(8,128)(2,1)} copy(bf16[2048,1024]{1,0:T(8,128)(2,1)} %all-gather.13.cloned.1.call-done) | data formatting | bytes 8388608 | tf_op jit(solution)/shard_map/all_gather | solution.py:98
  423.8 3.7 copy.48
  427.5 2.6 multiply_reduce_fusion
  (55 shorter events, 14.3 us)
Async XLA Ops:
  7.2 158.5 %copy-start = (bf16[256,4096]{1,0:T(8,128)(2,1)S(1)}, bf16[256,4096]{1,0:T(8,128)(2,1)}, u32[]{:S(2)}) copy-start(bf16[256,4096]{1,0:T(8,128)(2,1)} %param.13) | copy-start | bytes 6291460
  7.2 80.6 %all-gather.9.cloned.1.call-start = ((), (), s32[]{:S(2)}) async-start(), calls=%async_computation.2 | async-start | bytes 2228224 | tf_op jit(solution)/shard_map/all_gather | solution.py:45
  11.8 1.3 copy-start.5
  15.5 4.6 %copy-start.6 = (bf16[1,256,1024]{2,1,0:T(8,128)(2,1)S(1)}, bf16[1,256,1024]{2,1,0:T(8,128)(2,1)}, u32[]{:S(2)}) copy-start(bf16[1,256,1024]{2,1,0:T(8,128)(2,1)} %param.16) | copy-start | bytes 1572868
  16.2 145.2 %all-gather.7.cloned.1.call-start = ((), (), s32[]{:S(2)}) async-start(), calls=%async_computation.1 | async-start | bytes 2228224 | tf_op jit(solution)/shard_map/all_gather | solution.py:46
  24.4 236.9 %all-to-all-start = ((bf16[16,1,256,1024]{3,2,1,0:T(8,128)(2,1)}), bf16[16,1,256,1024]{3,2,1,0:T(8,128)(2,1)}, u32[]{:S(2)}, u32[]{:S(2)}) async-start(bf16[16,1,256,1024]{3,2,1,0:T(8,128)(2,1)} %stack.2), calls=%async_computation | async-start | bytes 16777216 | tf_op jit(solution)/shard_map/all_to_all | solution.py:77
  31.2 226.4 %all-reduce.2.cloned.1.call-start = ((), (), s32[]{:S(2)}) async-start(), calls=%async_computation.3 | async-start | bytes 4194304 | tf_op jit(solution)/shard_map/psum | solution.py:72
  90.4 1.9 copy-start.3
  165.5 2.5 copy-start.7
  167.7 89.9 %copy-start.2 = (bf16[2,128,4096]{2,1,0:T(8,128)(2,1)S(1)}, bf16[2,128,4096]{2,1,0:T(8,128)(2,1)}, u32[]{:S(2)}) copy-start(bf16[2,128,4096]{2,1,0:T(8,128)(2,1)} %param.10) | copy-start | bytes 6291460
  167.7 178.0 %all-gather.11.cloned.1.call-start = ((), (), s32[]{:S(2)}) async-start(), calls=%async_computation.4 | async-start | bytes 4718592 | tf_op jit(solution)/shard_map/all_gather | solution.py:97
  261.3 6.5 %copy-start.8 = (f32[1,1024]{1,0:T(1,128)S(1)}, f32[1,1024]{1,0:T(1,128)}, u32[]{:S(2)}) copy-start(f32[1,1024]{1,0:T(1,128)} %param.17) | copy-start | bytes 12292
  270.9 146.3 %all-gather.13.cloned.1.call-start = ((), (), s32[]{:S(2)}) async-start(), calls=%async_computation.5 | async-start | bytes 4718592 | tf_op jit(solution)/shard_map/all_gather | solution.py:98
  427.4 2.8 copy-start.4
  427.5 4.3 copy-start.1
Sparse Core Ops, SparseCore 0:
  16.3 71.4 all-gather.8
  90.0 71.3 all-gather.6
  167.8 89.7 all-reduce.1
  271.1 74.6 all-gather.10
  347.9 69.2 all-gather.12
